TPU v7x, 32 devices: a whole 2x2x4 slice. The times are simulated.
32 devices in a mesh: fsdp: 16 (over z, y, x), tp: 2 (over core).
Axes of the slice: x: 2, y: 2, z: 4, core: 2. Of those that a mesh axis runs over, the one named last changes fastest.
Arguments:
- images: bfloat16 [256, 197, 384], P('fsdp'), may hold values from -6 to 6
- cotangent: bfloat16 [256, 197, 384], P('fsdp'), may hold values from -0.02734375 to 0.02734375
- image_count: int32 [16, 2], P('fsdp'), may hold values from 1 to 8, as said below
- w_qkv: bfloat16 [2, 384, 3, 384], P(None, 'fsdp', None, 'tp'), may hold values from -0.3125 to 0.3125
- w_out: bfloat16 [2, 384, 384], P(None, 'tp', 'fsdp'), may hold values from -1.25 to 1.25
- w_up: bfloat16 [2, 384, 1536], P(None, 'fsdp', 'tp'), may hold values from -0.3125 to 0.3125
- w_down: bfloat16 [2, 1536, 384], P(None, 'tp', 'fsdp'), may hold values from -0.15625 to 0.15625
- vectors: bfloat16 [2, 6, 384], P(None, None, 'fsdp'), may hold values from -2 to 2, as said below
- head_bias: bfloat16 [2, 2, 6, 64], P(None, None, 'tp', 'fsdp'), may hold values from -3 to 3
- up_bias: bfloat16 [2, 24, 64], P(None, 'tp', 'fsdp'), may hold values from -3 to 3
- qkv_moments: float32 [2, 2, 384, 3, 384], P(None, None, 'fsdp', None, 'tp'), may hold values from -0.3 to 0.3, as said below
- out_moments: float32 [2, 2, 384, 384], P(None, None, 'tp', 'fsdp'), may hold values from -0.3 to 0.3, as said below
- up_moments: float32 [2, 2, 384, 1536], P(None, None, 'fsdp', 'tp'), may hold values from -0.3 to 0.3, as said below
- down_moments: float32 [2, 2, 1536, 384], P(None, None, 'tp', 'fsdp'), may hold values from -0.3 to 0.3, as said below
- vector_moments: float32 [2, 2, 6, 384], P(None, None, None, 'fsdp'), may hold values from -0.3 to 0.3, as said below
- head_bias_moments: float32 [2, 2, 2, 6, 64], P(None, None, None, 'tp', 'fsdp'), may hold values from -0.3 to 0.3, as said below
- up_bias_moments: float32 [2, 2, 24, 64], P(None, None, 'tp', 'fsdp'), may hold values from -0.3 to 0.3, as said below
Outputs:
- out_acts: float32 [256, 197, 384], P('fsdp')
- input_grad: float32 [256, 197, 384], P('fsdp')
- grad_qkv: float32 [2, 384, 3, 384], P(None, 'fsdp', None, 'tp')
- grad_out: float32 [2, 384, 384], P(None, 'tp', 'fsdp')
- grad_up: float32 [2, 384, 1536], P(None, 'fsdp', 'tp')
- grad_down: float32 [2, 1536, 384], P(None, 'tp', 'fsdp')
- grad_vectors: float32 [2, 6, 384], P(None, None, 'fsdp')
- grad_head_bias: float32 [2, 2, 6, 64], P(None, None, 'tp', 'fsdp')
- grad_up_bias: float32 [2, 24, 64], P(None, 'tp', 'fsdp')
- new_qkv_moments: float32 [2, 2, 384, 3, 384], P(None, None, 'fsdp', None, 'tp')
- new_out_moments: float32 [2, 2, 384, 384], P(None, None, 'tp', 'fsdp')
- new_up_moments: float32 [2, 2, 384, 1536], P(None, None, 'fsdp', 'tp')
- new_down_moments: float32 [2, 2, 1536, 384], P(None, None, 'tp', 'fsdp')
- new_vector_moments: float32 [2, 2, 6, 384], P(None, None, None, 'fsdp')
- new_head_bias_moments: float32 [2, 2, 2, 6, 64], P(None, None, None, 'tp', 'fsdp')
- new_up_bias_moments: float32 [2, 2, 24, 64], P(None, None, 'tp', 'fsdp')
- update_qkv: float32 [2, 384, 3, 384], P(None, 'fsdp', None, 'tp')
- update_out: float32 [2, 384, 384], P(None, 'tp', 'fsdp')
- update_up: float32 [2, 384, 1536], P(None, 'fsdp', 'tp')
- update_down: float32 [2, 1536, 384], P(None, 'tp', 'fsdp')
- update_vectors: float32 [2, 6, 384], P(None, None, 'fsdp')
- update_head_bias: float32 [2, 2, 6, 64], P(None, None, 'tp', 'fsdp')
- update_up_bias: float32 [2, 24, 64], P(None, 'tp', 'fsdp')
Inputs may be any that keep to these rules, and one draw needn't show every extreme that they name: `image_count`: the live images of a group in a micro-batch are its first slots; in every micro-batch some group has all 8 slots live. `vectors`: rows 0 and 3 of each layer hold norm gains, the other rows shifts and biases. `qkv_moments`: index 0 holds first moments, index 1 positive second moments. `out_moments`: index 0 holds first moments, index 1 positive second moments. `up_moments`: index 0 holds first moments, index 1 positive second moments. `down_moments`: index 0 holds first moments, index 1 positive second moments. `vector_moments`: index 0 holds first moments, index 1 positive second moments. `head_bias_moments`: index 0 holds first moments, index 1 positive second moments. `up_bias_moments`: index 0 holds first moments, index 1 positive second moments.
All inputs are finite; a program needn't handle non-finite values.
Results may differ from a plain program's by a relative error of at most 0.024.
Values may be sent and summed in bfloat16 or wider, within the bound.
No kernel may reach another device: no remote copies, remote signals or barrier semaphores. Data moves between devices by JAX's collectives and lax.ppermute only.
A program may use at most 256 MiB of HBM per device.

v0:
```python
from functools import partial

import jax
import jax.numpy as jnp
from jax import lax
from jax.sharding import PartitionSpec as P

D = 384
HD = 64
SEQ = 197
LAYERS = 2
MICRO = 2
IMG_MB = 8
ADAM_STEP = 4
IMG_DEV = 16


EPS_NORM = 1e-06
LEARN_RATE = 0.05
BETA_ONE = 0.9
BETA_TWO = 0.95
ADAM_EPS = 1e-08
DECAY_RATE = 0.05


def norm_parts(values, gain_row, shift_row):
    centre = values - jnp.mean(values, axis=-1, keepdims=True)
    variance = jnp.mean(centre * centre, axis=-1, keepdims=True)
    inverse = lax.rsqrt(variance + EPS_NORM)
    scaled = centre * inverse
    return (scaled * gain_row + shift_row, scaled, inverse)


def norm_back(grad_normed, scaled, inverse, gain_row):
    grad_scaled = grad_normed * gain_row
    return inverse * (
        grad_scaled
        - jnp.mean(grad_scaled, axis=-1, keepdims=True)
        - scaled * jnp.mean(grad_scaled * scaled, axis=-1, keepdims=True)
    )


def token_sum(values):
    return jnp.sum(values, axis=(0, 1))


def layer_forward(stream, weights, reducers):
    qkv_weight, out_weight, up_weight, down_weight, vector_rows, head_biases, up_biases = weights
    vec_rows = vector_rows.astype(jnp.float32)
    batch_size, seq_len, width = stream.shape
    heads_here = head_biases.shape[1]
    normed, scaled_one, inverse_one = norm_parts(stream, vec_rows[0], vec_rows[1])
    normed_low = normed.astype(jnp.bfloat16)
    mixed_proj = jnp.einsum(
        "bsd,dkc->bskc", normed_low, qkv_weight, preferred_element_type=jnp.float32
    )
    bias_rows = head_biases.astype(jnp.float32).reshape(2, -1)
    query_low = (mixed_proj[:, :, 0] + bias_rows[0]).astype(jnp.bfloat16)
    keys_low = mixed_proj[:, :, 1].astype(jnp.bfloat16)
    values_low = (mixed_proj[:, :, 2] + bias_rows[1]).astype(jnp.bfloat16)
    head_shape = (batch_size, seq_len, heads_here, HD)
    scores = (
        jnp.einsum(
            "bqhe,bkhe->bhqk",
            query_low.reshape(head_shape),
            keys_low.reshape(head_shape),
            preferred_element_type=jnp.float32,
        )
        * 0.125
    )
    log_total = jax.nn.logsumexp(scores, axis=-1, keepdims=True)
    probs_low = jnp.exp(scores - log_total).astype(jnp.bfloat16)
    attended = jnp.einsum(
        "bhqk,bkhe->bqhe",
        probs_low,
        values_low.reshape(head_shape),
        preferred_element_type=jnp.float32,
    )
    attended_low = attended.reshape(batch_size, seq_len, heads_here * HD).astype(jnp.bfloat16)
    branch = jnp.einsum("bsc,cd->bsd", attended_low, out_weight, preferred_element_type=jnp.float32)
    branch = reducers[0](branch)
    middle = stream + branch + vec_rows[2]
    normed_two, scaled_two, inverse_two = norm_parts(middle, vec_rows[3], vec_rows[4])
    normed_two_low = normed_two.astype(jnp.bfloat16)
    hidden = jnp.einsum(
        "bsd,df->bsf", normed_two_low, up_weight, preferred_element_type=jnp.float32
    )
    hidden = hidden + up_biases.astype(jnp.float32).reshape(-1)
    activated_low = jax.nn.gelu(hidden, approximate=False).astype(jnp.bfloat16)
    branch_two = jnp.einsum(
        "bsf,fd->bsd", activated_low, down_weight, preferred_element_type=jnp.float32
    )
    branch_two = reducers[1](branch_two)
    result = middle + branch_two + vec_rows[5]
    cache = (
        scaled_one,
        inverse_one,
        normed_low,
        query_low,
        keys_low,
        values_low,
        log_total,
        attended_low,
        scaled_two,
        inverse_two,
        normed_two_low,
        hidden,
    )
    return (result, cache)


def layer_backward(grad_stream, weights, cache, reducers):
    qkv_weight, out_weight, up_weight, down_weight, vector_rows, head_biases, up_biases = weights
    (
        scaled_one,
        inverse_one,
        normed_low,
        query_low,
        keys_low,
        values_low,
        log_total,
        attended_low,
        scaled_two,
        inverse_two,
        normed_two_low,
        hidden,
    ) = cache
    vec_rows = vector_rows.astype(jnp.float32)
    batch_size, seq_len, width = grad_stream.shape
    heads_here = head_biases.shape[1]
    head_shape = (batch_size, seq_len, heads_here, HD)
    grad_mlp_bias = token_sum(grad_stream)
    grad_stream_low = grad_stream.astype(jnp.bfloat16)
    activated, gelu_back = jax.vjp(partial(jax.nn.gelu, approximate=False), hidden)
    activated_low = activated.astype(jnp.bfloat16)
    grad_down_w = jnp.einsum(
        "bsf,bsd->fd", activated_low, grad_stream_low, preferred_element_type=jnp.float32
    )
    grad_act = jnp.einsum(
        "bsd,fd->bsf", grad_stream_low, down_weight, preferred_element_type=jnp.float32
    )
    grad_hidden_low = gelu_back(grad_act)[0].astype(jnp.bfloat16)
    grad_up_b = token_sum(grad_hidden_low.astype(jnp.float32)).reshape(up_biases.shape)
    grad_up_w = jnp.einsum(
        "bsd,bsf->df", normed_two_low, grad_hidden_low, preferred_element_type=jnp.float32
    )
    grad_normed_two = jnp.einsum(
        "bsf,df->bsd", grad_hidden_low, up_weight, preferred_element_type=jnp.float32
    )
    grad_normed_two = reducers[2](grad_normed_two)
    grad_gain_two = token_sum(grad_normed_two * scaled_two)
    grad_shift_two = token_sum(grad_normed_two)
    grad_middle = grad_stream + norm_back(grad_normed_two, scaled_two, inverse_two, vec_rows[3])
    grad_out_bias = token_sum(grad_middle)
    grad_middle_low = grad_middle.astype(jnp.bfloat16)
    grad_out_w = jnp.einsum(
        "bsc,bsd->cd", attended_low, grad_middle_low, preferred_element_type=jnp.float32
    )
    grad_att_low = (
        jnp.einsum("bsd,cd->bsc", grad_middle_low, out_weight, preferred_element_type=jnp.float32)
        .astype(jnp.bfloat16)
        .reshape(head_shape)
    )
    query_heads = query_low.reshape(head_shape)
    keys_heads = keys_low.reshape(head_shape)
    values_heads = values_low.reshape(head_shape)
    scores = (
        jnp.einsum("bqhe,bkhe->bhqk", query_heads, keys_heads, preferred_element_type=jnp.float32)
        * 0.125
    )
    probs = jnp.exp(scores - log_total)
    probs_low = probs.astype(jnp.bfloat16)
    grad_probs = jnp.einsum(
        "bqhe,bkhe->bhqk", grad_att_low, values_heads, preferred_element_type=jnp.float32
    )
    grad_values = jnp.einsum(
        "bhqk,bqhe->bkhe", probs_low, grad_att_low, preferred_element_type=jnp.float32
    )
    grad_scores_low = (
        probs * (grad_probs - jnp.sum(grad_probs * probs, axis=-1, keepdims=True))
    ).astype(jnp.bfloat16)
    grad_query = (
        jnp.einsum(
            "bhqk,bkhe->bqhe", grad_scores_low, keys_heads, preferred_element_type=jnp.float32
        )
        * 0.125
    )
    grad_keys = (
        jnp.einsum(
            "bhqk,bqhe->bkhe", grad_scores_low, query_heads, preferred_element_type=jnp.float32
        )
        * 0.125
    )
    flat_shape = (batch_size, seq_len, heads_here * HD)
    grad_mixed_low = jnp.stack(
        [
            grad_query.reshape(flat_shape),
            grad_keys.reshape(flat_shape),
            grad_values.reshape(flat_shape),
        ],
        axis=2,
    ).astype(jnp.bfloat16)
    grad_head_b = jnp.stack(
        [
            token_sum(grad_mixed_low[:, :, 0].astype(jnp.float32)),
            token_sum(grad_mixed_low[:, :, 2].astype(jnp.float32)),
        ]
    ).reshape(head_biases.shape)
    grad_qkv_w = jnp.einsum(
        "bsd,bskc->dkc", normed_low, grad_mixed_low, preferred_element_type=jnp.float32
    )
    grad_normed = jnp.einsum(
        "bskc,dkc->bsd", grad_mixed_low, qkv_weight, preferred_element_type=jnp.float32
    )
    grad_normed = reducers[3](grad_normed)
    grad_gain_one = token_sum(grad_normed * scaled_one)
    grad_shift_one = token_sum(grad_normed)
    grad_input = grad_middle + norm_back(grad_normed, scaled_one, inverse_one, vec_rows[0])
    grad_vec = jnp.stack(
        [grad_gain_one, grad_shift_one, grad_out_bias, grad_gain_two, grad_shift_two, grad_mlp_bias]
    )
    return (
        grad_input,
        (grad_qkv_w, grad_out_w, grad_up_w, grad_down_w, grad_vec, grad_head_b, grad_up_b),
    )


def adam_step(weight_now, gradient, moments):
    first_moment = BETA_ONE * moments[0] + (1.0 - BETA_ONE) * gradient
    second_moment = BETA_TWO * moments[1] + (1.0 - BETA_TWO) * gradient * gradient
    first_fix = first_moment / (1.0 - BETA_ONE**ADAM_STEP)
    second_fix = second_moment / (1.0 - BETA_TWO**ADAM_STEP)
    change = -LEARN_RATE * (
        first_fix / (jnp.sqrt(second_fix) + ADAM_EPS) + DECAY_RATE * weight_now.astype(jnp.float32)
    )
    return (jnp.stack([first_moment, second_moment]), change)


def per_device(
    images,
    cotangent,
    image_count,
    w_qkv,
    w_out,
    w_up,
    w_down,
    vectors,
    head_bias,
    up_bias,
    qkv_moments,
    out_moments,
    up_moments,
    down_moments,
    vector_moments,
    head_bias_moments,
    up_bias_moments,
):

    def sum_heads(values):
        return lax.psum(values, "tp")

    def sum_hidden(values):
        return lax.psum(values.astype(jnp.bfloat16), "tp").astype(jnp.float32)

    def sum_mlp_grad(values):
        return lax.psum(values, "tp")

    def sum_attn_grad(values):
        return lax.psum(values.astype(jnp.bfloat16), "tp").astype(jnp.float32)

    reducers = (sum_heads, sum_hidden, sum_mlp_grad, sum_attn_grad)
    q_weights, o_weights, u_weights, d_weights, hb_weights, ub_weights = (
        w_qkv,
        w_out,
        w_up,
        w_down,
        head_bias,
        up_bias,
    )
    slots_here = IMG_MB
    cols_here = q_weights.shape[3]
    hidden_here = u_weights.shape[2]
    heads_here = hb_weights.shape[2]
    groups_here = ub_weights.shape[1]
    grad_totals = []
    for layer_idx in range(LAYERS):
        grad_totals.append(
            (
                jnp.zeros((D, 3, cols_here), jnp.float32),
                jnp.zeros((cols_here, D), jnp.float32),
                jnp.zeros((D, hidden_here), jnp.float32),
                jnp.zeros((hidden_here, D), jnp.float32),
                jnp.zeros((6, D), jnp.float32),
                jnp.zeros((2, heads_here, HD), jnp.float32),
                jnp.zeros((groups_here, HD), jnp.float32),
            )
        )
    outputs_list = []
    grads_list = []
    for micro_idx in range(MICRO):
        first_image = micro_idx * IMG_MB
        slot_ids = jnp.arange(slots_here, dtype=jnp.int32)
        live_mask = (slot_ids < image_count[0, micro_idx]).astype(jnp.float32)[:, None, None]
        stream = lax.dynamic_slice_in_dim(images, first_image, slots_here, 0).astype(jnp.float32)
        caches = []
        for layer_idx in range(LAYERS):
            stream, cache = layer_forward(
                stream,
                (
                    lax.all_gather(q_weights[layer_idx], "fsdp", axis=0, tiled=True),
                    lax.all_gather(o_weights[layer_idx], "fsdp", axis=1, tiled=True),
                    lax.all_gather(u_weights[layer_idx], "fsdp", axis=0, tiled=True),
                    lax.all_gather(d_weights[layer_idx], "fsdp", axis=1, tiled=True),
                    lax.all_gather(vectors[layer_idx], "fsdp", axis=1, tiled=True),
                    lax.all_gather(hb_weights[layer_idx], "fsdp", axis=2, tiled=True),
                    lax.all_gather(ub_weights[layer_idx], "fsdp", axis=1, tiled=True),
                ),
                reducers,
            )
            caches.append(cache)
        outputs_list.append(stream * live_mask)
        grad_stream = (
            lax.dynamic_slice_in_dim(cotangent, first_image, slots_here, 0).astype(jnp.float32)
            * live_mask
        )
        for layer_idx in reversed(range(LAYERS)):
            grad_stream, layer_grads = layer_backward(
                grad_stream,
                (
                    lax.all_gather(q_weights[layer_idx], "fsdp", axis=0, tiled=True),
                    lax.all_gather(o_weights[layer_idx], "fsdp", axis=1, tiled=True),
                    lax.all_gather(u_weights[layer_idx], "fsdp", axis=0, tiled=True),
                    lax.all_gather(d_weights[layer_idx], "fsdp", axis=1, tiled=True),
                    lax.all_gather(vectors[layer_idx], "fsdp", axis=1, tiled=True),
                    lax.all_gather(hb_weights[layer_idx], "fsdp", axis=2, tiled=True),
                    lax.all_gather(ub_weights[layer_idx], "fsdp", axis=1, tiled=True),
                ),
                caches[layer_idx],
                reducers,
            )
            grad_totals[layer_idx] = tuple(
                (left + right for left, right in zip(grad_totals[layer_idx], layer_grads))
            )
        grads_list.append(grad_stream)
    out_local = jnp.stack(outputs_list)
    grad_local = jnp.stack(grads_list)
    stacked = [
        jnp.stack([grad_totals[layer_idx][index_p] for layer_idx in range(LAYERS)])
        for index_p in range(7)
    ]
    stack_qkv, stack_out, stack_up, stack_down, stack_vec, stack_head, stack_upb = stacked
    owned = (
        lax.psum_scatter(stack_qkv, "fsdp", scatter_dimension=1, tiled=True),
        lax.psum_scatter(stack_out, "fsdp", scatter_dimension=2, tiled=True),
        lax.psum_scatter(stack_up, "fsdp", scatter_dimension=1, tiled=True),
        lax.psum_scatter(stack_down, "fsdp", scatter_dimension=2, tiled=True),
        lax.psum_scatter(stack_vec, "fsdp", scatter_dimension=2, tiled=True),
        lax.psum_scatter(stack_head, "fsdp", scatter_dimension=3, tiled=True),
        lax.psum_scatter(stack_upb, "fsdp", scatter_dimension=2, tiled=True),
    )
    out_acts = out_local.reshape(IMG_DEV, SEQ, D)
    input_grad = grad_local.reshape(IMG_DEV, SEQ, D)
    param_list = (w_qkv, w_out, w_up, w_down, vectors, head_bias, up_bias)
    moment_list = (
        qkv_moments,
        out_moments,
        up_moments,
        down_moments,
        vector_moments,
        head_bias_moments,
        up_bias_moments,
    )
    new_moments = []
    updates = []
    for index_p in range(7):
        moved, change = adam_step(param_list[index_p], owned[index_p], moment_list[index_p])
        new_moments.append(moved)
        updates.append(change)
    return (
        out_acts,
        input_grad,
        owned[0],
        owned[1],
        owned[2],
        owned[3],
        owned[4],
        owned[5],
        owned[6],
        new_moments[0],
        new_moments[1],
        new_moments[2],
        new_moments[3],
        new_moments[4],
        new_moments[5],
        new_moments[6],
        updates[0],
        updates[1],
        updates[2],
        updates[3],
        updates[4],
        updates[5],
        updates[6],
    )


def solution(mesh):
    placed = (
        P("fsdp", None, None),
        P("fsdp", None, None),
        P("fsdp", None),
        P(None, "fsdp", None, "tp"),
        P(None, "tp", "fsdp"),
        P(None, "fsdp", "tp"),
        P(None, "tp", "fsdp"),
        P(None, None, "fsdp"),
        P(None, None, "tp", "fsdp"),
        P(None, "tp", "fsdp"),
        P(None, None, "fsdp", None, "tp"),
        P(None, None, "tp", "fsdp"),
        P(None, None, "fsdp", "tp"),
        P(None, None, "tp", "fsdp"),
        P(None, None, None, "fsdp"),
        P(None, None, None, "tp", "fsdp"),
        P(None, None, "tp", "fsdp"),
    )
    return jax.shard_map(
        per_device,
        mesh=mesh,
        in_specs=placed,
        out_specs=(
            P("fsdp", None, None),
            P("fsdp", None, None),
            P(None, "fsdp", None, "tp"),
            P(None, "tp", "fsdp"),
            P(None, "fsdp", "tp"),
            P(None, "tp", "fsdp"),
            P(None, None, "fsdp"),
            P(None, None, "tp", "fsdp"),
            P(None, "tp", "fsdp"),
            P(None, None, "fsdp", None, "tp"),
            P(None, None, "tp", "fsdp"),
            P(None, None, "fsdp", "tp"),
            P(None, None, "tp", "fsdp"),
            P(None, None, None, "fsdp"),
            P(None, None, None, "tp", "fsdp"),
            P(None, None, "tp", "fsdp"),
            P(None, "fsdp", None, "tp"),
            P(None, "tp", "fsdp"),
            P(None, "fsdp", "tp"),
            P(None, "tp", "fsdp"),
            P(None, None, "fsdp"),
            P(None, None, "tp", "fsdp"),
            P(None, "tp", "fsdp"),
        ),
        check_vma=False,
    )
```

profile of v0, /device:TPU:0, one launch (start us, length us, event | category | flops | bytes accessed | tf_op | source)
XLA Modules:
  0.0 1350.9 jit_solution(7795214804478089615)
XLA Ops:
  10.8 43.4 %all-gather = bf16[1,6,384]{1,0,2:T(2,128)(2,1)S(1)} all-gather(bf16[1,6,24]{1,0,2:T(2,128)(2,1)S(1)} %copy.461), channel_id=2, replica_groups=mesh['fsdp'=16,'tp'=2] {'fsdp'}, dimensions={2}, use_global_device_ids=true | all-gather | bytes 4896 | tf_op jit(solution)/shard_map/all_gather | solution.py:314
  54.4 8.3 slice_reduce_fusion.6
  62.8 38.9 %all-gather.1 = bf16[1,384,3,192]{3,1,2,0:T(8,128)(2,1)S(1)} all-gather(bf16[1,24,3,192]{3,1,2,0:T(8,128)(2,1)S(1)} %get-tuple-element.292), channel_id=3, replica_groups=mesh['fsdp'=16,'tp'=2] {'fsdp'}, dimensions={1}, use_global_device_ids=true | all-gather | bytes 470016 | tf_op jit(solution)/shard_map/all_gather | solution.py:310
  111.2 37.8 %all-gather.2 = bf16[1,2,3,64]{2,1,0,3:T(2,128)(2,1)S(1)} all-gather(bf16[1,2,3,4]{2,1,0,3:T(2,128)(2,1)S(1)} %copy.462), channel_id=4, replica_groups=mesh['fsdp'=16,'tp'=2] {'fsdp'}, dimensions={3}, use_global_device_ids=true | all-gather | bytes 816 | tf_op jit(solution)/shard_map/all_gather | solution.py:315
  154.1 36.6 %all-gather.3 = bf16[1,192,384]{1,2,0:T(8,128)(2,1)S(1)} all-gather(bf16[1,192,24]{1,2,0:T(8,128)(2,1)S(1)} %get-tuple-element.300), channel_id=5, replica_groups=mesh['fsdp'=16,'tp'=2] {'fsdp'}, dimensions={2}, use_global_device_ids=true | all-gather | bytes 156672 | tf_op jit(solution)/shard_map/all_gather | solution.py:311
  203.2 38.3 %all-gather.5 = bf16[1,12,64]{1,0,2:T(2,128)(2,1)S(1)} all-gather(bf16[1,12,4]{1,0,2:T(2,128)(2,1)S(1)} %copy.463), channel_id=7, replica_groups=mesh['fsdp'=16,'tp'=2] {'fsdp'}, dimensions={2}, use_global_device_ids=true | all-gather | bytes 1632 | tf_op jit(solution)/shard_map/all_gather | solution.py:316
  242.9 39.0 %all-gather.4 = bf16[1,384,768]{2,1,0:T(8,128)(2,1)S(1)} all-gather(bf16[1,24,768]{2,1,0:T(8,128)(2,1)S(1)} %get-tuple-element.290), channel_id=6, replica_groups=mesh['fsdp'=16,'tp'=2] {'fsdp'}, dimensions={1}, use_global_device_ids=true | all-gather | bytes 626688 | tf_op jit(solution)/shard_map/all_gather | solution.py:312
  281.9 42.9 %all-gather.6 = bf16[1,768,384]{1,2,0:T(8,128)(2,1)} all-gather(bf16[1,768,24]{1,2,0:T(8,128)(2,1)S(1)} %get-tuple-element.288), channel_id=8, replica_groups=mesh['fsdp'=16,'tp'=2] {'fsdp'}, dimensions={2}, use_global_device_ids=true | all-gather | bytes 626688 | tf_op jit(solution)/shard_map/all_gather | solution.py:313
  336.7 23.8 %multiply_convert_fusion.7 = (bf16[8,197,768]{2,1,0:T(8,128)(2,1)S(1)}, f32[8,197,768]{2,1,0:T(8,128)}, bf16[8,197,768]{2,1,0:T(8,128)(2,1)S(1)}, f32[8,197,768]{2,1,0:T(8,128)}) fusion(f32[8,197,768]{2,1,0:T(8,128)S(1)} %get-tuple-element.344, f32[768]{0:T(1024)S(1)} %reshape.958, u8[197,768]{1,0:T(8,128)(4,1)S(1)} %get-tuple-element.149, ...), kind=kLoop, calls=%fused_computation.88 | loop fusion | flops 170661888 | bytes 24815616 | tf_op jit(solution)/shard_map/convert_element_type | solution.py:89
  365.9 36.5 %all-gather.7 = bf16[1,6,384]{1,0,2:T(2,128)(2,1)S(1)} all-gather(bf16[1,6,24]{1,0,2:T(2,128)(2,1)S(1)} %copy.464), channel_id=9, replica_groups=mesh['fsdp'=16,'tp'=2] {'fsdp'}, dimensions={2}, use_global_device_ids=true | all-gather | bytes 4896 | tf_op jit(solution)/shard_map/all_gather | solution.py:314
  402.7 37.7 %all-gather.9 = bf16[1,2,3,64]{2,1,0,3:T(2,128)(2,1)S(1)} all-gather(bf16[1,2,3,4]{2,1,0,3:T(2,128)(2,1)S(1)} %copy.465), channel_id=11, replica_groups=mesh['fsdp'=16,'tp'=2] {'fsdp'}, dimensions={3}, use_global_device_ids=true | all-gather | bytes 816 | tf_op jit(solution)/shard_map/all_gather | solution.py:315
  441.2 36.5 %all-gather.10 = bf16[1,192,384]{1,2,0:T(8,128)(2,1)S(1)} all-gather(bf16[1,192,24]{1,2,0:T(8,128)(2,1)S(1)} %get-tuple-element.299), channel_id=12, replica_groups=mesh['fsdp'=16,'tp'=2] {'fsdp'}, dimensions={2}, use_global_device_ids=true | all-gather | bytes 156672 | tf_op jit(solution)/shard_map/all_gather | solution.py:311
  477.7 41.1 %all-gather.8 = bf16[1,384,3,192]{3,1,2,0:T(8,128)(2,1)S(1)} all-gather(bf16[1,24,3,192]{3,1,2,0:T(8,128)(2,1)S(1)} %get-tuple-element.291), channel_id=10, replica_groups=mesh['fsdp'=16,'tp'=2] {'fsdp'}, dimensions={1}, use_global_device_ids=true | all-gather | bytes 470016 | tf_op jit(solution)/shard_map/all_gather | solution.py:310
  518.8 8.8 slice_reduce_fusion
  548.0 36.6 %all-gather.12 = bf16[1,12,64]{1,0,2:T(2,128)(2,1)S(1)} all-gather(bf16[1,12,4]{1,0,2:T(2,128)(2,1)S(1)} %copy.466), channel_id=14, replica_groups=mesh['fsdp'=16,'tp'=2] {'fsdp'}, dimensions={2}, use_global_device_ids=true | all-gather | bytes 1632 | tf_op jit(solution)/shard_map/all_gather | solution.py:316
  590.4 42.3 %all-gather.11 = bf16[1,384,768]{2,1,0:T(8,128)(2,1)} all-gather(bf16[1,24,768]{2,1,0:T(8,128)(2,1)S(1)} %copy-done.157), channel_id=13, replica_groups=mesh['fsdp'=16,'tp'=2] {'fsdp'}, dimensions={1}, use_global_device_ids=true | all-gather | bytes 626688 | tf_op jit(solution)/shard_map/all_gather | solution.py:312
  632.7 42.0 %all-gather.13 = bf16[1,768,384]{1,2,0:T(8,128)(2,1)} all-gather(bf16[1,768,24]{1,2,0:T(8,128)(2,1)} %get-tuple-element.287), channel_id=15, replica_groups=mesh['fsdp'=16,'tp'=2] {'fsdp'}, dimensions={2}, use_global_device_ids=true | all-gather | bytes 626688 | tf_op jit(solution)/shard_map/all_gather | solution.py:313
  688.8 24.1 %multiply_convert_fusion.6 = (bf16[8,197,768]{2,1,0:T(8,128)(2,1)}, f32[8,197,768]{2,1,0:T(8,128)S(1)}, bf16[8,197,768]{2,1,0:T(8,128)(2,1)}, f32[8,197,768]{2,1,0:T(8,128)S(1)}) fusion(f32[8,197,768]{2,1,0:T(8,128)S(1)} %get-tuple-element.349, f32[768]{0:T(1024)S(1)} %copy-done.206, u8[197,768]{1,0:T(8,128)(4,1)S(1)} %get-tuple-element.147, ...), kind=kLoop, calls=%fused_computation.73 | loop fusion | flops 170661888 | bytes 24815616 | tf_op jit(solution)/shard_map/convert_element_type | solution.py:89
  727.8 26.4 %all-reduce.28.cloned.1.call-done = (f32[8,197,384]{2,1,0:T(8,128)}, f32[8,197,384]{2,1,0:T(8,128)}) async-done(((f32[8,197,384]{2,1,0:T(8,128)}, f32[8,197,384]{2,1,0:T(8,128)}), (f32[8,197,384]{2,1,0:T(8,128)}, f32[8,197,384]{2,1,0:T(8,128)})) %all-reduce.28.cloned.1.call-update) | async-done | bytes 4841488 | tf_op jit(solution)/shard_map/psum | solution.py:266
  797.7 15.1 %all-reduce.36.cloned.1.call-done = (bf16[8,197,384]{2,1,0:T(8,128)(2,1)}, bf16[8,197,384]{2,1,0:T(8,128)(2,1)}) async-done(((bf16[8,197,384]{2,1,0:T(8,128)(2,1)}, bf16[8,197,384]{2,1,0:T(8,128)(2,1)}), (bf16[8,197,384]{2,1,0:T(8,128)(2,1)}, bf16[8,197,384]{2,1,0:T(8,128)(2,1)})) %all-reduce.36.cloned.1.call-update) | async-done | bytes 2420752 | tf_op jit(solution)/shard_map/psum | solution.py:269
  975.5 34.2 %reduce-scatter.4.cloned.1.call-done = f32[2,24,768]{2,1,0:T(8,128)} async-done(((f32[2,384,768]{2,1,0:T(8,128)}), f32[2,24,768]{2,1,0:T(8,128)}) %reduce-scatter.4.cloned.1.call-update) | async-done | bytes 147472 | tf_op jit(solution)/shard_map/reduce_scatter | solution.py:355
  1025.6 184.3 %all-reduce.24.cloned.1.call-done = (f32[2,384,3,192]{3,0,2,1:T(2,128)}, f32[2,192,384]{1,0,2:T(2,128)}, f32[2,768,384]{1,0,2:T(2,128)}) async-done(((f32[2,384,3,192]{3,0,2,1:T(2,128)}, f32[2,192,384]{1,0,2:T(2,128)}, f32[2,768,384]{1,0,2:T(2,128)}), (f32[2,384,3,192]{3,0,2,1:T(2,128)}, f32[2,192,384]{1,0,2:T(2,128)}, f32[2,768,384]{1,0,2:T(2,128)})) %all-reduce.24.cloned.1.call-update) | async-done | bytes 4718608
  1221.4 20.0 %all-reduce.34.cloned.1.call-done = (bf16[8,197,384]{2,1,0:T(8,128)(2,1)}, bf16[8,197,384]{2,1,0:T(8,128)(2,1)}, bf16[8,197,384]{2,1,0:T(8,128)(2,1)}, bf16[8,197,384]{2,1,0:T(8,128)(2,1)}) async-done(((bf16[8,197,384]{2,1,0:T(8,128)(2,1)}, bf16[8,197,384]{2,1,0:T(8,128)(2,1)}, bf16[8,197,384]{2,1,0:T(8,128)(2,1)}, bf16[8,197,384]{2,1,0:T(8,128)(2,1)}), (bf16[8,197,384]{2,1,0:T(8,128)(2,1)}, ...) | async-done | bytes 4841488 | tf_op jit(solution)/shard_map/psum | solution.py:263
  1250.0 78.1 %all-reduce.6 = (f32[2,6,384]{2,0,1:T(2,128)S(1)}, f32[2,2,3,64]{3,1,2,0:T(2,128)S(1)}, f32[2,12,64]{1,0,2:T(2,128)S(1)}) all-reduce(f32[2,6,384]{2,0,1:T(2,128)S(1)} %pad_maximum_fusion.22, f32[2,2,3,64]{3,1,2,0:T(2,128)S(1)} %copy-done.198, f32[2,12,64]{1,0,2:T(2,128)S(1)} %copy-done.152), channel_id=20, replica_groups=mesh['fsdp'=16,'tp'=2] {'fsdp'}, use_global_device_ids=true, to_apply=%region_88.0.clone | all-reduce | flops 6912 | bytes 55296
  (813 shorter events, 359.7 us)
Async XLA Ops:
  7.2 317.6 %all-reduce.32.cloned.1.call-start = ((), (), s32[]{:S(2)}) async-start(), calls=%async_computation.6 | async-start | bytes 9830400 | tf_op jit(solution)/shard_map/psum | solution.py:260
  9.1 92.6 %copy-start.22 = (bf16[8,197,384]{2,0,1:T(8,128)(2,1)}, bf16[8,197,384]{2,0,1:T(8,128)(2,1)S(1)}, u32[]{:S(2)}) copy-start(bf16[8,197,384]{2,0,1:T(8,128)(2,1)S(1)} %get-tuple-element.270) | copy-start | bytes 3631108
  9.1 97.6 %copy-start.20 = (bf16[8,197,384]{2,0,1:T(8,128)(2,1)}, bf16[8,197,384]{2,0,1:T(8,128)(2,1)S(1)}, u32[]{:S(2)}) copy-start(bf16[8,197,384]{2,0,1:T(8,128)(2,1)S(1)} %get-tuple-element.271) | copy-start | bytes 3631108
  9.8 93.5 %copy-start.163 = (f32[8,197]{1,0:T(8,128)}, f32[8,197]{1,0:T(8,128)S(1)}, u32[]{:S(2)}) copy-start(f32[8,197]{1,0:T(8,128)S(1)} %broadcast_multiply_fusion.23) | copy-start | bytes 18916
  10.6 92.7 %copy-start.175 = (f32[8,197]{1,0:T(8,128)}, f32[8,197]{1,0:T(8,128)S(1)}, u32[]{:S(2)}) copy-start(f32[8,197]{1,0:T(8,128)S(1)} %add_rsqrt_fusion.7) | copy-start | bytes 18916
  62.8 269.0 %copy-start.153 = (f32[384]{0:T(512)}, f32[384]{0:T(512)S(1)}, u32[]{:S(2)}) copy-start(f32[384]{0:T(512)S(1)} %get-tuple-element.186) | copy-start | bytes 4612
  62.8 269.0 %copy-start.158 = (f32[384]{0:T(512)}, f32[384]{0:T(512)S(1)}, u32[]{:S(2)}) copy-start(f32[384]{0:T(512)S(1)} %get-tuple-element.185) | copy-start | bytes 4612
  104.9 89.5 %copy-start.37 = (f32[8,197,1,192]{1,3,2,0:T(8,128)}, f32[8,197,1,192]{1,3,2,0:T(8,128)S(1)}, u32[]{:S(2)}) copy-start(f32[8,197,1,192]{1,3,2,0:T(8,128)S(1)} %get-tuple-element.264) | copy-start | bytes 3631108
  201.9 325.6 %all-reduce.38.cloned.1.call-start = ((), (), s32[]{:S(2)}) async-start(), calls=%async_computation.9 | async-start | bytes 4915200 | tf_op jit(solution)/shard_map/psum | solution.py:263
  241.7 95.0 %copy-start.204 = (f32[768]{0:T(1024)}, f32[768]{0:T(1024)S(1)}, u32[]{:S(2)}) copy-start(f32[768]{0:T(1024)S(1)} %reshape.958) | copy-start | bytes 9220
  328.9 198.7 %copy-start.4 = (f32[8,197,384]{2,1,0:T(8,128)}, f32[8,197,384]{2,1,0:T(8,128)S(1)}, u32[]{:S(2)}) copy-start(f32[8,197,384]{2,1,0:T(8,128)S(1)} %get-tuple-element.337) | copy-start | bytes 7262212
  365.7 310.6 %all-reduce.30.cloned.1.call-start = ((), (), s32[]{:S(2)}) async-start(), calls=%async_computation.5 | async-start | bytes 9830400 | tf_op jit(solution)/shard_map/psum | solution.py:260
  440.6 96.0 %copy-start.184 = (f32[1,1,3,64]{3,2,1,0:T(4,128)}, f32[1,1,3,64]{3,2,1,0:T(4,128)S(1)}, u32[]{:S(2)}) copy-start(f32[1,1,3,64]{3,2,1,0:T(4,128)S(1)} %copy.358) | copy-start | bytes 2308
  547.3 127.4 %copy-start.112 = (bf16[16,197,384]{2,0,1:T(8,128)(2,1)S(1)}, bf16[16,197,384]{2,0,1:T(8,128)(2,1)}, u32[]{:S(2)}) copy-start(bf16[16,197,384]{2,0,1:T(8,128)(2,1)} %param.18) | copy-start | bytes 7262212
  547.3 206.9 %all-reduce.28.cloned.1.call-start = ((), (), s32[]{:S(2)}) async-start(), calls=%async_computation.4 | async-start | bytes 9830400 | tf_op jit(solution)/shard_map/psum | solution.py:266
  680.9 114.0 %copy-start.6 = (f32[8,197,384]{2,1,0:T(8,128)}, f32[8,197,384]{2,1,0:T(8,128)S(1)}, u32[]{:S(2)}) copy-start(f32[8,197,384]{2,1,0:T(8,128)S(1)} %get-tuple-element.331) | copy-start | bytes 7262212
  727.7 85.1 %all-reduce.36.cloned.1.call-start = ((), (), s32[]{:S(2)}) async-start(), calls=%async_computation.8 | async-start | bytes 4915200 | tf_op jit(solution)/shard_map/psum | solution.py:269
  789.5 89.4 %all-reduce.26.cloned.1.call-start = ((), (), s32[]{:S(2)}) async-start(), calls=%async_computation.3 | async-start | bytes 9830400 | tf_op jit(solution)/shard_map/psum | solution.py:266
  843.4 166.3 %reduce-scatter.4.cloned.1.call-start = ((), (), s32[]{:S(2)}) async-start(), calls=%async_computation.1 | async-start | bytes 2506752 | tf_op jit(solution)/shard_map/reduce_scatter | solution.py:355
  878.8 331.0 %all-reduce.24.cloned.1.call-start = ((), (), s32[]{:S(2)}) async-start(), calls=%async_computation.2 | async-start | bytes 11010048
  928.5 312.9 %all-reduce.34.cloned.1.call-start = ((), (), s32[]{:S(2)}) async-start(), calls=%async_computation.7 | async-start | bytes 9830400 | tf_op jit(solution)/shard_map/psum | solution.py:263
  1022.8 190.5 %copy-start.140 = (f32[1,2,192,24]{2,3,1,0:T(8,128)S(1)}, f32[1,2,192,24]{2,3,1,0:T(8,128)}, u32[]{:S(2)}) copy-start(f32[1,2,192,24]{2,3,1,0:T(8,128)} %get-tuple-element.286) | copy-start | bytes 110596
  1022.8 190.5 %copy-start.171 = (bf16[2,192,24]{1,2,0:T(8,128)(2,1)S(1)}, bf16[2,192,24]{1,2,0:T(8,128)(2,1)}, u32[]{:S(2)}) copy-start(bf16[2,192,24]{1,2,0:T(8,128)(2,1)} %param.21) | copy-start | bytes 55300
  1022.8 192.2 %copy-start.148 = (bf16[2,24,3,192]{3,1,2,0:T(8,128)(2,1)S(1)}, bf16[2,24,3,192]{3,1,2,0:T(8,128)(2,1)}, u32[]{:S(2)}) copy-start(bf16[2,24,3,192]{3,1,2,0:T(8,128)(2,1)} %param.20) | copy-start | bytes 165892
  (234 other events, 2250.3 us)
Sparse Core Ops, SparseCore 0:
  202.1 26.9 all-reduce.31
  365.8 17.8 all-reduce.37
  547.5 25.5 all-reduce.29
  727.9 26.3 all-reduce.27
  789.6 23.1 all-reduce.35
  843.5 30.3 all-reduce.25
  879.4 130.2 reduce-scatter.3
  1016.7 193.0 all-reduce.23
  1212.6 28.7 all-reduce.33
where the time goes:
time: 1360 us; the launch traced here: 1350 us
  blocking collectives  628 us (46%)
  waiting for transfers between devices  280 us (21%)
  other arithmetic  167 us (12%)
  matrix products  147 us (11%)
  local copies, waits for them, and re-layouts  109 us (8%)
  between operations  18.5 us (1%)
    unnamed x10, waiting for transfers between devices  184 us
    all_gather x2, blocking collectives, per_device(): lax.all_gather(d_weights[layer_idx], 'fsdp', axis=1, tiled=True)  84.9 us
    all_gather x2, blocking collectives, per_device(): lax.all_gather(u_weights[layer_idx], 'fsdp', axis=0, tiled=True)  81.3 us
    all_gather x2, blocking collectives, per_device(): lax.all_gather(vectors[layer_idx], 'fsdp', axis=1, tiled=True)  80 us
    all_gather x2, blocking collectives, per_device(): lax.all_gather(q_weights[layer_idx], 'fsdp', axis=0, tiled=True)  79.9 us
    unnamed x1, blocking collectives  78.1 us
    all_gather x2, blocking collectives, per_device(): lax.all_gather(hb_weights[layer_idx], 'fsdp', axis=2, tiled=True)  75.5 us
    all_gather x2, blocking collectives, per_device(): lax.all_gather(ub_weights[layer_idx], 'fsdp', axis=1, tiled=True)  74.8 us
  transfers between devices with their start and end apart: 9, of which 5 were waited for; matrix products, arithmetic and copies ran while one was open for 13% of the time, Pallas kernels for 0%

commit v1 on v0

--- a/solution.py
+++ b/solution.py
@@ -236,7 +236,80 @@
     return (jnp.stack([first_moment, second_moment]), change)
 
 
+def radix_bits(count):
+    bits = []
+    while (1 << len(bits)) < count:
+        bits.append(1 << len(bits))
+    return bits
+
+
+def swap_with(values, bit, axis, size):
+    return lax.ppermute(values, axis, [(dev, dev ^ bit) for dev in range(size)])
+
+
+def gather_order(size, swap_tail):
+    bits = radix_bits(size)
+    tail = bits[:2]
+    if swap_tail:
+        tail = tail[::-1]
+    return bits[2:] + tail
+
+
+def gather_rows(shard, size, swap_tail):
+    index = lax.axis_index("fsdp")
+    done = []
+    block = shard[None]
+    for bit in gather_order(size, swap_tail):
+        other = swap_with(block, bit, "fsdp", size)
+        high = (index & bit) != 0
+        first = jnp.where(high, other, block)
+        second = jnp.where(high, block, other)
+        done.append(bit)
+        done.sort(reverse=True)
+        place = done.index(bit)
+        lead = 1 << place
+        rest = block.shape[0] // lead
+        shape = (lead, rest) + shard.shape
+        block = jnp.stack([first.reshape(shape), second.reshape(shape)], axis=1)
+        block = block.reshape((lead * 2 * rest,) + shard.shape)
+    return block
+
+
+def scatter_rows(full, size, swap_tail):
+    index = lax.axis_index("fsdp")
+    left = sorted(radix_bits(size), reverse=True)
+    block = full
+    for bit in gather_order(size, swap_tail)[::-1]:
+        place = left.index(bit)
+        lead = 1 << place
+        rest = block.shape[0] // lead // 2
+        split = block.reshape((lead, 2, rest) + full.shape[1:])
+        high = (index & bit) != 0
+        keep = jnp.where(high, split[:, 1], split[:, 0])
+        send = jnp.where(high, split[:, 0], split[:, 1]).astype(jnp.bfloat16)
+        got = swap_with(send, bit, "fsdp", size)
+        block = (keep + got.astype(jnp.float32)).reshape((lead * rest,) + full.shape[1:])
+        left.remove(bit)
+    return block[0]
+
+
+def swap_cores(values):
+    return lax.ppermute(values, "tp", [(0, 1), (1, 0)])
+
+
+def pack_small(vectors, head_bias, up_bias):
+    rows = up_bias.shape[0] * up_bias.shape[1]
+    vec = vectors.reshape(-1, vectors.shape[-1])
+    hb = head_bias.reshape(-1, head_bias.shape[-1])
+    ub = up_bias.reshape(-1, up_bias.shape[-1])
+    vec = jnp.pad(vec, ((0, rows - vec.shape[0]), (0, 0)))
+    hb = jnp.pad(hb, ((0, rows - hb.shape[0]), (0, 0)))
+    small = jnp.concatenate([vec, hb, ub], axis=1)
+    return jnp.pad(small, ((0, 0), (0, 128 - small.shape[1])))
+
+
 def per_device(
+    sizes,
     images,
     cotangent,
     image_count,
@@ -255,111 +328,120 @@
     head_bias_moments,
     up_bias_moments,
 ):
-
-    def sum_heads(values):
-        return lax.psum(values, "tp")
-
-    def sum_hidden(values):
-        return lax.psum(values.astype(jnp.bfloat16), "tp").astype(jnp.float32)
-
-    def sum_mlp_grad(values):
-        return lax.psum(values, "tp")
-
-    def sum_attn_grad(values):
-        return lax.psum(values.astype(jnp.bfloat16), "tp").astype(jnp.float32)
-
-    reducers = (sum_heads, sum_hidden, sum_mlp_grad, sum_attn_grad)
-    q_weights, o_weights, u_weights, d_weights, hb_weights, ub_weights = (
-        w_qkv,
-        w_out,
-        w_up,
-        w_down,
-        head_bias,
-        up_bias,
-    )
-    slots_here = IMG_MB
-    cols_here = q_weights.shape[3]
-    hidden_here = u_weights.shape[2]
-    heads_here = hb_weights.shape[2]
-    groups_here = ub_weights.shape[1]
-    grad_totals = []
-    for layer_idx in range(LAYERS):
-        grad_totals.append(
-            (
-                jnp.zeros((D, 3, cols_here), jnp.float32),
-                jnp.zeros((cols_here, D), jnp.float32),
-                jnp.zeros((D, hidden_here), jnp.float32),
-                jnp.zeros((hidden_here, D), jnp.float32),
-                jnp.zeros((6, D), jnp.float32),
-                jnp.zeros((2, heads_here, HD), jnp.float32),
-                jnp.zeros((groups_here, HD), jnp.float32),
+    fsdp = sizes
+    core = lax.axis_index("tp")
+    rows = w_qkv.shape[1]
+    heads_here = head_bias.shape[2]
+    groups_here = up_bias.shape[1]
+    cols = w_qkv.shape[3]
+    hidden = w_up.shape[2]
+    dv, dh, du = vectors.shape[2], head_bias.shape[3], up_bias.shape[2]
+
+    small = gather_rows(pack_small(vectors, head_bias, up_bias), fsdp, False)
+    small_two = swap_cores(small)
+
+    def vec_of(block):
+        return block[:, :12, :dv].transpose(1, 0, 2).reshape(LAYERS, 6, D)
+
+    def hb_of(block):
+        part = block[:, : 4 * heads_here, dv : dv + dh]
+        return part.transpose(1, 0, 2).reshape(LAYERS, 2, heads_here, HD)
+
+    def ub_of(block):
+        part = block[:, :, dv + dh : dv + dh + du]
+        return part.transpose(1, 0, 2).reshape(LAYERS, groups_here, HD)
+
+    vec_full = vec_of(small)
+    hb_full = jnp.concatenate([hb_of(small), hb_of(small_two)], axis=2)
+    ub_full = jnp.concatenate([ub_of(small), ub_of(small_two)], axis=1)
+
+    layer_weights = []
+    for l in range(LAYERS):
+        attn = jnp.concatenate([w_qkv[l].reshape(rows, 3 * cols), w_out[l].T], axis=1)
+        halves = []
+        for part, tail in ((attn, False), (w_up[l], True), (w_down[l].T, False)):
+            own = gather_rows(part, fsdp, tail).reshape(D, -1)
+            halves.append((own, swap_cores(own)))
+        attn_h, up_h, down_h = halves
+        q_full = jnp.concatenate([h[:, : 3 * cols].reshape(D, 3, cols) for h in attn_h], axis=2)
+        o_full = jnp.concatenate([h[:, 3 * cols :] for h in attn_h], axis=1).T
+        u_full = jnp.concatenate(up_h, axis=1)
+        d_full = jnp.concatenate(down_h, axis=1).T
+        layer_weights.append((q_full, o_full, u_full, d_full, vec_full[l], hb_full[l], ub_full[l]))
+
+    reducers = (lambda v: v,) * 4
+    first = core * IMG_MB
+    live = (jnp.arange(IMG_MB, dtype=jnp.int32) < image_count[0, core]).astype(jnp.float32)
+    live_mask = live[:, None, None]
+    stream = lax.dynamic_slice_in_dim(images, first, IMG_MB, 0).astype(jnp.float32)
+    caches = []
+    for l in range(LAYERS):
+        stream, cache = layer_forward(stream, layer_weights[l], reducers)
+        caches.append(cache)
+    out_own = stream * live_mask
+    grad_stream = (
+        lax.dynamic_slice_in_dim(cotangent, first, IMG_MB, 0).astype(jnp.float32) * live_mask
+    )
+    owned_layers = [None] * LAYERS
+    small_grads = [None] * LAYERS
+    for l in reversed(range(LAYERS)):
+        grad_stream, grads = layer_backward(grad_stream, layer_weights[l], caches[l], reducers)
+        gq, go, gu, gd, gv, gh, gb = grads
+        own_other = []
+        for h in range(2):
+            c = slice(h * cols, (h + 1) * cols)
+            f = slice(h * hidden, (h + 1) * hidden)
+            own_other.append(
+                (
+                    jnp.concatenate([gq[:, :, c].reshape(D, 3 * cols), go[c].T], axis=1),
+                    gu[:, f],
+                    gd[f].T,
+                )
             )
-        )
-    outputs_list = []
-    grads_list = []
-    for micro_idx in range(MICRO):
-        first_image = micro_idx * IMG_MB
-        slot_ids = jnp.arange(slots_here, dtype=jnp.int32)
-        live_mask = (slot_ids < image_count[0, micro_idx]).astype(jnp.float32)[:, None, None]
-        stream = lax.dynamic_slice_in_dim(images, first_image, slots_here, 0).astype(jnp.float32)
-        caches = []
-        for layer_idx in range(LAYERS):
-            stream, cache = layer_forward(
-                stream,
-                (
-                    lax.all_gather(q_weights[layer_idx], "fsdp", axis=0, tiled=True),
-                    lax.all_gather(o_weights[layer_idx], "fsdp", axis=1, tiled=True),
-                    lax.all_gather(u_weights[layer_idx], "fsdp", axis=0, tiled=True),
-                    lax.all_gather(d_weights[layer_idx], "fsdp", axis=1, tiled=True),
-                    lax.all_gather(vectors[layer_idx], "fsdp", axis=1, tiled=True),
-                    lax.all_gather(hb_weights[layer_idx], "fsdp", axis=2, tiled=True),
-                    lax.all_gather(ub_weights[layer_idx], "fsdp", axis=1, tiled=True),
-                ),
-                reducers,
-            )
-            caches.append(cache)
-        outputs_list.append(stream * live_mask)
-        grad_stream = (
-            lax.dynamic_slice_in_dim(cotangent, first_image, slots_here, 0).astype(jnp.float32)
-            * live_mask
-        )
-        for layer_idx in reversed(range(LAYERS)):
-            grad_stream, layer_grads = layer_backward(
-                grad_stream,
-                (
-                    lax.all_gather(q_weights[layer_idx], "fsdp", axis=0, tiled=True),
-                    lax.all_gather(o_weights[layer_idx], "fsdp", axis=1, tiled=True),
-                    lax.all_gather(u_weights[layer_idx], "fsdp", axis=0, tiled=True),
-                    lax.all_gather(d_weights[layer_idx], "fsdp", axis=1, tiled=True),
-                    lax.all_gather(vectors[layer_idx], "fsdp", axis=1, tiled=True),
-                    lax.all_gather(hb_weights[layer_idx], "fsdp", axis=2, tiled=True),
-                    lax.all_gather(ub_weights[layer_idx], "fsdp", axis=1, tiled=True),
-                ),
-                caches[layer_idx],
-                reducers,
-            )
-            grad_totals[layer_idx] = tuple(
-                (left + right for left, right in zip(grad_totals[layer_idx], layer_grads))
-            )
-        grads_list.append(grad_stream)
-    out_local = jnp.stack(outputs_list)
-    grad_local = jnp.stack(grads_list)
-    stacked = [
-        jnp.stack([grad_totals[layer_idx][index_p] for layer_idx in range(LAYERS)])
-        for index_p in range(7)
-    ]
-    stack_qkv, stack_out, stack_up, stack_down, stack_vec, stack_head, stack_upb = stacked
+        owned = []
+        for own, other, tail in zip(own_other[0], own_other[1], (False, True, False)):
+            got = swap_cores(other.astype(jnp.bfloat16)).astype(jnp.float32)
+            summed = (own + got).reshape(fsdp, rows, -1)
+            owned.append(scatter_rows(summed, fsdp, tail))
+        owned_layers[l] = owned
+        small_grads[l] = (gv, gh, gb)
+    gv = jnp.stack([small_grads[l][0] for l in range(LAYERS)])
+    gh = jnp.stack([small_grads[l][1] for l in range(LAYERS)])
+    gb = jnp.stack([small_grads[l][2] for l in range(LAYERS)])
+
+    def small_pack(h):
+        hsl = slice(h * heads_here, (h + 1) * heads_here)
+        gsl = slice(h * groups_here, (h + 1) * groups_here)
+        nrow = LAYERS * groups_here
+        a = gv.reshape(12, fsdp, dv).transpose(1, 0, 2)
+        b = gh[:, :, hsl].reshape(4 * heads_here, fsdp, dh).transpose(1, 0, 2)
+        c = gb[:, gsl].reshape(nrow, fsdp, du).transpose(1, 0, 2)
+        a = jnp.pad(a, ((0, 0), (0, nrow - a.shape[1]), (0, 0)))
+        b = jnp.pad(b, ((0, 0), (0, nrow - b.shape[1]), (0, 0)))
+        packed = jnp.concatenate([a, b, c], axis=2)
+        return jnp.pad(packed, ((0, 0), (0, 0), (0, 128 - packed.shape[2])))
+
+    small_sum = scatter_rows(small_pack(0) + swap_cores(small_pack(1)), fsdp, False)
+    g_vec = small_sum[:12, :dv].reshape(LAYERS, 6, dv)
+    g_hb = small_sum[: 4 * heads_here, dv : dv + dh].reshape(LAYERS, 2, heads_here, dh)
+    g_ub = small_sum[:, dv + dh : dv + dh + du].reshape(LAYERS, groups_here, du)
     owned = (
-        lax.psum_scatter(stack_qkv, "fsdp", scatter_dimension=1, tiled=True),
-        lax.psum_scatter(stack_out, "fsdp", scatter_dimension=2, tiled=True),
-        lax.psum_scatter(stack_up, "fsdp", scatter_dimension=1, tiled=True),
-        lax.psum_scatter(stack_down, "fsdp", scatter_dimension=2, tiled=True),
-        lax.psum_scatter(stack_vec, "fsdp", scatter_dimension=2, tiled=True),
-        lax.psum_scatter(stack_head, "fsdp", scatter_dimension=3, tiled=True),
-        lax.psum_scatter(stack_upb, "fsdp", scatter_dimension=2, tiled=True),
-    )
-    out_acts = out_local.reshape(IMG_DEV, SEQ, D)
-    input_grad = grad_local.reshape(IMG_DEV, SEQ, D)
+        jnp.stack([o[0][:, : 3 * cols].reshape(rows, 3, cols) for o in owned_layers]),
+        jnp.stack([o[0][:, 3 * cols :].T for o in owned_layers]),
+        jnp.stack([o[1] for o in owned_layers]),
+        jnp.stack([o[2].T for o in owned_layers]),
+        g_vec,
+        g_hb,
+        g_ub,
+    )
+
+    def both(own):
+        other = swap_cores(own)
+        low = core == 0
+        return jnp.concatenate([jnp.where(low, own, other), jnp.where(low, other, own)])
+
+    out_acts = both(out_own)
+    input_grad = both(grad_stream)
     param_list = (w_qkv, w_out, w_up, w_down, vectors, head_bias, up_bias)
     moment_list = (
         qkv_moments,
@@ -376,31 +458,7 @@
         moved, change = adam_step(param_list[index_p], owned[index_p], moment_list[index_p])
         new_moments.append(moved)
         updates.append(change)
-    return (
-        out_acts,
-        input_grad,
-        owned[0],
-        owned[1],
-        owned[2],
-        owned[3],
-        owned[4],
-        owned[5],
-        owned[6],
-        new_moments[0],
-        new_moments[1],
-        new_moments[2],
-        new_moments[3],
-        new_moments[4],
-        new_moments[5],
-        new_moments[6],
-        updates[0],
-        updates[1],
-        updates[2],
-        updates[3],
-        updates[4],
-        updates[5],
-        updates[6],
-    )
+    return (out_acts, input_grad, *owned, *new_moments, *updates)
 
 
 def solution(mesh):
@@ -424,7 +482,7 @@
         P(None, None, "tp", "fsdp"),
     )
     return jax.shard_map(
-        per_device,
+        partial(per_device, mesh.shape["fsdp"]),
         mesh=mesh,
         in_specs=placed,
         out_specs=(

time: 1360 us -> 586 us (0.43)
  blocking collectives: 628 us -> 0 us
  waiting for transfers between devices: 280 us -> 63.3 us
  starting transfers between devices: 1.24 us -> 72.5 us
  matrix products: 147 us -> 184 us
  other arithmetic: 167 us -> 133 us
  between operations: 18.5 us -> 4.23 us
    all_gather x14 -> x0, blocking collectives: 550 us -> none  [the longest x2 84.9 us: per_device(): lax.all_gather(d_weights[layer_idx], 'fsdp', axis=1, tiled=True)]
    unnamed x10 -> x0, waiting for transfers between devices: 184 us -> none
    unnamed x1 -> x0, blocking collectives: 78.1 us -> none
    ppermute x0 -> x72, starting transfers between devices: none -> 72.5 us  [the longest x56 68.8 us: swap_with(): return lax.ppermute(values, axis, [(dev, dev ^ bit) for dev in range(size)])]
    ppermute x0 -> x72, waiting for transfers between devices: none -> 63.3 us  [the longest x56 63.3 us: swap_with(): return lax.ppermute(values, axis, [(dev, dev ^ bit) for dev in range(size)])]
    psum x7 -> x0, waiting for transfers between devices: 61.6 us -> none  [the longest x2 26.5 us: sum_mlp_grad(): return lax.psum(values, 'tp')]
    reduce_sum x19 -> x7, other arithmetic: 54 us -> 6.54 us  [token_sum(): return jnp.sum(values, axis=(0, 1))]
    reduce_scatter x1 -> x0, waiting for transfers between devices: 34.2 us -> none  [per_device(): lax.psum_scatter(stack_up, 'fsdp', scatter_dimension=1, tiled=True)]
  transfers between devices with their start and end apart: 9 -> 72, of which waited for: 5 -> 25; matrix products, arithmetic and copies ran while one was open for 13% -> 43% of each run, Pallas kernels for 0% -> 0%
where the time goes in v1:
time: 586 us; the launch traced here: 576 us
  matrix products  184 us (31%)
  other arithmetic  133 us (23%)
  local copies, waits for them, and re-layouts  119 us (20%)
  starting transfers between devices  72.5 us (12%)
  waiting for transfers between devices  63.3 us (11%)
    ppermute x56, starting transfers between devices, swap_with(): return lax.ppermute(values, axis, [(dev, dev ^ bit) for dev in range(size)])  68.8 us
    ppermute x56, waiting for transfers between devices, swap_with(): return lax.ppermute(values, axis, [(dev, dev ^ bit) for dev in range(size)])  63.3 us
    convert_element_type x2, other arithmetic, layer_forward(): activated_low = jax.nn.gelu(hidden, approximate=False).astype(jnp.bfloat16)  56.4 us
    unnamed x296, local copies, waits for them, and re-layouts  25.5 us
    convert_element_type x2, other arithmetic, layer_backward(): grad_scores_low = (probs * (grad_probs - jnp.sum(grad_probs * probs, axis...  23.8 us
    dot_general x2, matrix products, layer_backward(): jnp.einsum('bqhe,bkhe->bhqk', grad_att_low, values_heads, preferred_eleme...  22.3 us
    dot_general x2, matrix products, layer_backward(): jnp.einsum('bsd,fd->bsf', grad_stream_low, down_weight, preferred_element...  20.6 us
    dot_general x2, matrix products, layer_forward(): jnp.einsum('bhqk,bkhe->bqhe', probs_low, values_low.reshape(head_shape),...  13.9 us
  transfers between devices with their start and end apart: 72, of which 25 were waited for; matrix products, arithmetic and copies ran while one was open for 43% of the time, Pallas kernels for 0%

profile of v1, /device:TPU:0, one launch (start us, length us, event | category | flops | bytes accessed | tf_op | source)
XLA Modules:
  0.0 576.2 jit_solution(8668215812702150294)
XLA Ops:
  66.9 6.5 %collective-permute-done.7 = bf16[8,24,768]{2,1,0:T(8,128)(2,1)S(1)} collective-permute-done((bf16[8,24,768]{2,1,0:T(8,128)(2,1)S(1)}, bf16[8,24,768]{2,1,0:T(8,128)(2,1)S(1)}, u32[]{:S(2)}, u32[]{:S(2)}) %collective-permute-start.7) | collective-permute-done | bytes 294944 | tf_op jit(solution)/shard_map/ppermute | solution.py:247
  74.3 5.5 collective-permute-done.23
  108.8 7.8 %multiply_reduce_fusion.3 = (f32[8,6,197]{2,1,0:T(8,128)S(1)}, f32[8,6,197,197]{2,3,1,0:T(8,128)}) fusion(bf16[8,197,6,64]{1,3,2,0:T(8,128)(2,1)} %bitcast.993, f32[8,197,6,64]{1,3,2,0:T(8,128)} %bitcast.987, f32[6,64]{1,0:T(8,128)S(1)} %get-tuple-element.360), kind=kOutput, calls=%fused_computation.52 | convolution fusion | flops 243369072 | bytes 11121792 | tf_op jit(solution)/shard_map/bqhe,bkhe->bhqk/dot_general | solution.py:63
  120.0 5.8 %exponential_reduce_fusion.1 = f32[8,6,197]{2,1,0:T(8,128)S(1)} fusion(f32[8,6,197,197]{2,3,1,0:T(8,128)} %get-tuple-element.327, f32[8,6,197]{2,1,0:T(8,128)S(1)} %is-finite_select_fusion.1), kind=kLoop, calls=%fused_computation.50 | loop fusion | flops 5579040 | bytes 7526976 | tf_op jit(solution)/shard_map/reduce_sum | solution.py:71
  129.1 6.9 %convolution_convert_fusion.3 = bf16[8,6,64,197]{3,2,1,0:T(8,128)(2,1)S(1)} fusion(f32[8,6,197,197]{2,3,1,0:T(8,128)} %get-tuple-element.327, f32[8,6,197]{2,1,0:T(8,128)S(1)} %log_add_fusion.1, f32[8,197,6,64]{1,3,2,0:T(8,128)} %bitcast.983, f32[6,64]{1,0:T(8,128)S(1)} %get-tuple-element.361), kind=kOutput, calls=%fused_computation.139 | convolution fusion | flops 245846544 | bytes 11121792 | tf_op jit(solution)/shard_map/bhqk,bkhe->bqhe/dot_general | solution.py:73
  141.3 6.6 %fusion.34 = (u8[197,1536]{1,0:T(8,128)(4,1)S(1)}, u8[197,1536]{1,0:T(8,128)(4,1)S(1)}, f32[8,197,1536]{2,1,0:T(8,128)S(1)}) fusion(f32[1536]{0:T(1024)S(1)} %reshape.2099, bf16[384,768]{1,0:T(8,128)(2,1)} %collective-permute-done.14, bf16[384,768]{1,0:T(8,128)(2,1)} %bitcast.59, f32[8,197,384]{2,1,0:T(8,128)S(1)} %get-tuple-element.329, ...), kind=kOutput, calls=%fused_computation.123 | convolution fusion | flops 1897795584 | bytes 13910336 | tf_op jit(solution)/shard_map/bsd,df->bsf/dot_general | solution.py:85
  147.9 32.6 %multiply_convert_fusion.3 = (bf16[8,197,1536]{2,1,0:T(8,128)(2,1)S(1)}, f32[8,197,1536]{2,1,0:T(8,128)}) fusion(f32[8,197,1536]{2,1,0:T(8,128)S(1)} %get-tuple-element.330, f32[1536]{0:T(1024)S(1)} %reshape.2099, u8[197,1536]{1,0:T(8,128)(4,1)S(1)} %get-tuple-element.141, u8[197,1536]{1,0:T(8,128)(4,1)S(1)} %get-tuple-element.140), kind=kLoop, calls=%fused_computation.36 | loop fusion | flops 171872256 | bytes 24818688 | tf_op jit(solution)/shard_map/convert_element_type | solution.py:89
  210.3 7.0 %convolution_convert_fusion.2 = bf16[8,6,64,197]{3,2,1,0:T(8,128)(2,1)S(1)} fusion(f32[8,6,197,197]{2,3,1,0:T(8,128)} %copy-done.2, f32[8,6,197]{2,1,0:T(8,128)S(1)} %log_add_fusion, f32[8,197,6,64]{1,3,2,0:T(8,128)} %bitcast.985, f32[6,64]{1,0:T(8,128)S(1)} %get-tuple-element.316), kind=kOutput, calls=%fused_computation.138 | convolution fusion | flops 245846544 | bytes 11121792 | tf_op jit(solution)/shard_map/bhqk,bkhe->bqhe/dot_general | solution.py:73
  219.5 6.7 %fusion.35 = (u8[197,1536]{1,0:T(8,128)(4,1)S(1)}, u8[197,1536]{1,0:T(8,128)(4,1)S(1)}, f32[8,197,1536]{2,1,0:T(8,128)S(1)}) fusion(f32[1536]{0:T(1024)S(1)} %reshape.2100, bf16[384,768]{1,0:T(8,128)(2,1)} %collective-permute-done.29, bf16[384,768]{1,0:T(8,128)(2,1)} %bitcast.124, f32[8,197,384]{2,1,0:T(8,128)S(1)} %get-tuple-element.336, ...), kind=kOutput, calls=%fused_computation.124 | convolution fusion | flops 1897795584 | bytes 13910336 | tf_op jit(solution)/shard_map/bsd,df->bsf/dot_general | solution.py:85
  226.3 23.8 %multiply_convert_fusion.2 = (bf16[8,197,1536]{2,1,0:T(8,128)(2,1)}, f32[8,197,1536]{2,1,0:T(8,128)}) fusion(f32[8,197,1536]{2,1,0:T(8,128)S(1)} %get-tuple-element.337, f32[1536]{0:T(1024)S(1)} %reshape.2100, u8[197,1536]{1,0:T(8,128)(4,1)S(1)} %get-tuple-element.139, u8[197,1536]{1,0:T(8,128)(4,1)S(1)} %get-tuple-element.138), kind=kLoop, calls=%fused_computation.21 | loop fusion | flops 171872256 | bytes 24818688 | tf_op jit(solution)/shard_map/convert_element_type | solution.py:89
  250.1 9.8 %convert_reduce_fusion = (f32[1536]{0:T(1024)}, bf16[8,197,1536]{2,1,0:T(8,128)(2,1)S(1)}) fusion(f32[8,197,1536]{2,1,0:T(8,128)} %get-tuple-element.173, bf16[384,768]{1,0:T(8,128)(2,1)} %collective-permute-done.34, bf16[384,768]{1,0:T(8,128)(2,1)} %bitcast.145, f32[8]{0:T(128)S(1)} %copy-done.120, bf16[8,197,384]{2,0,1:T(8,128)(2,1)S(1)} %copy-done.45, ...), kind=kOutput, calls=%fused_computation.13 | convolution fusion | flops 1904451072 | bytes 26609696 | tf_op jit(solution)/shard_map/bsd,fd->bsf/dot_general | solution.py:139
  259.9 6.3 %multiply_reduce_fusion.4 = (f32[384]{0:T(512)}, f32[8,197]{1,0:T(8,128)S(1)}, f32[8,197]{1,0:T(8,128)S(1)}, f32[384]{0:T(512)}, f32[8,197,384]{2,1,0:T(8,128)S(1)}) fusion(f32[8,197,384]{2,1,0:T(8,128)S(1)} %get-tuple-element.336, f32[8,197]{1,0:T(8,128)S(1)} %add_rsqrt_fusion, f32[8,197]{1,0:T(8,128)S(1)} %broadcast_multiply_fusion.8, ...), kind=kOutput, calls=%fused_computation.101 | convolution fusion | flops 1866927360 | bytes 10892416 | tf_op jit(solution)/shard_map/bsf,df->bsd/dot_general | solution.py:147
  272.7 10.4 %multiply_reduce_fusion.1 = (f32[8,6,197]{2,1,0:T(8,128)S(1)}, f32[8,6,197,197]{2,3,1,0:T(8,128)}) fusion(f32[8,6,197,197]{2,3,1,0:T(8,128)} %copy-done.2, f32[8,6,197]{2,1,0:T(8,128)S(1)} %log_add_fusion, bf16[8,197,6,64]{1,3,2,0:T(8,128)(2,1)S(1)} %bitcast.1001, f32[8,197,6,64]{1,3,2,0:T(8,128)} %bitcast.986, f32[6,64]{1,0:T(8,128)S(1)} %get-tuple-element.316), kind=kOutput, calls=%fused_computation.19 | convolution fusion | flops 247094736 | bytes 18610944 | tf_op jit(solution)/shard_map/bqhe,bkhe->bhqk/dot_general | solution.py:173
  283.1 12.1 %multiply_convert_fusion.1 = bf16[8,6,197,197]{2,3,1,0:T(8,128)(2,1)} fusion(f32[8,6,197,197]{2,3,1,0:T(8,128)} %get-tuple-element.340, f32[8,6,197,197]{2,3,1,0:T(8,128)} %copy-done.2, f32[8,6,197]{2,1,0:T(8,128)S(1)} %get-tuple-element.339, f32[8,6,197]{2,1,0:T(8,128)S(1)} %log_add_fusion), kind=kLoop, calls=%fused_computation.18 | loop fusion | flops 9314160 | bytes 18703968 | tf_op jit(solution)/shard_map/convert_element_type | solution.py:181
  299.5 5.5 multiply_convert_fusion.6
  314.8 5.8 fusion.29
  321.8 10.8 %convert_reduce_fusion.1 = (f32[1536]{0:T(1024)S(1)}, bf16[8,197,1536]{2,1,0:T(8,128)(2,1)S(1)}) fusion(f32[8,197,1536]{2,1,0:T(8,128)} %get-tuple-element.175, bf16[384,768]{1,0:T(8,128)(2,1)} %collective-permute-done.19, bf16[384,768]{1,0:T(8,128)(2,1)} %bitcast.81, f32[8,197,384]{2,1,0:T(8,128)S(1)} %get-tuple-element.167, ...), kind=kOutput, calls=%fused_computation.14 | convolution fusion | flops 1903240704 | bytes 27820032 | tf_op jit(solution)/shard_map/bsd,fd->bsf/dot_general | solution.py:139
  332.6 5.7 multiply_reduce_fusion.5
  346.0 11.9 %multiply_reduce_fusion = (f32[8,6,197]{2,1,0:T(8,128)S(1)}, f32[8,6,197,197]{2,3,1,0:T(8,128)}) fusion(f32[8,6,197,197]{2,3,1,0:T(8,128)} %get-tuple-element.327, f32[8,6,197]{2,1,0:T(8,128)S(1)} %log_add_fusion.1, bf16[8,197,6,64]{1,3,2,0:T(8,128)(2,1)} %bitcast.1003, f32[8,197,6,64]{1,3,2,0:T(8,128)} %bitcast.984, f32[6,64]{1,0:T(8,128)S(1)} %get-tuple-element.361), kind=kOutput, calls=%fused_computation.16 | convolution fusion | flops 247094736 | bytes 18610944 | tf_op jit(solution)/shard_map/bqhe,bkhe->bhqk/dot_general | solution.py:173
  358.0 11.7 %multiply_convert_fusion = bf16[8,6,197,197]{2,3,1,0:T(8,128)(2,1)} fusion(f32[8,6,197,197]{2,3,1,0:T(8,128)} %get-tuple-element.344, f32[8,6,197,197]{2,3,1,0:T(8,128)} %get-tuple-element.327, f32[8,6,197]{2,1,0:T(8,128)S(1)} %get-tuple-element.343, f32[8,6,197]{2,1,0:T(8,128)S(1)} %log_add_fusion.1), kind=kLoop, calls=%fused_computation.15 | loop fusion | flops 9314160 | bytes 18703968 | tf_op jit(solution)/shard_map/convert_element_type | solution.py:181
  374.0 6.1 %multiply_convert_fusion.4 = bf16[8,6,64,197]{3,2,1,0:T(8,128)(2,1)} fusion(bf16[8,6,197,197]{2,3,1,0:T(8,128)(2,1)S(1)} %copy-done.4, f32[8,197,6,64]{1,3,2,0:T(8,128)} %bitcast.988, f32[6,64]{1,0:T(8,128)S(1)} %copy-done.89), kind=kOutput, calls=%fused_computation.66 | convolution fusion | flops 240863232 | bytes 7358304 | tf_op jit(solution)/shard_map/bhqk,bqhe->bkhe/dot_general | solution.py:189
  412.0 6.0 %fusion.26 = (f32[384]{0:T(512)S(1)}, f32[8,197]{1,0:T(8,128)S(1)}, f32[8,197]{1,0:T(8,128)S(1)}, f32[384]{0:T(512)S(1)}, f32[8,197,384,1]{2,1,3,0:T(8,128)}) fusion(f32[8,197]{1,0:T(8,128)S(1)} %copy-done.82, f32[8,197]{1,0:T(8,128)S(1)} %copy-done.77, bf16[8,197,384]{2,0,1:T(8,128)(2,1)S(1)} %copy-done.7, f32[384]{0:T(512)S(1)} %copy-done.93, ...), kind=kOutput, calls=%fused_computation.90 | convolution fusion | flops 1405792512 | bytes 8176768 | tf_op jit(solution)/shard_map/bskc,dkc->bsd/dot_general | solution.py:212
  436.8 5.6 add_multiply_fusion
  530.3 7.2 %collective-permute-done.65 = bf16[1,2,24,768]{3,2,1,0:T(8,128)(2,1)S(1)} collective-permute-done((bf16[1,2,24,768]{3,2,1,0:T(8,128)(2,1)S(1)}, bf16[1,2,24,768]{3,2,1,0:T(8,128)(2,1)S(1)}, u32[]{:S(2)}, u32[]{:S(2)}) %collective-permute-start.65) | collective-permute-done | bytes 73760 | tf_op jit(solution)/shard_map/ppermute | solution.py:247
  (817 shorter events, 347.9 us)
Async XLA Ops:
  2.6 22.7 %collective-permute-start.20 = (bf16[1,24,768]{2,1,0:T(8,128)(2,1)S(1)}, bf16[1,24,768]{2,1,0:T(8,128)(2,1)S(1)}, u32[]{:S(2)}, u32[]{:S(2)}) collective-permute-start(bf16[1,24,768]{2,1,0:T(8,128)(2,1)S(1)} %maximum_bitcast_fusion.31), channel_id=1, source_target_pairs={{0,8},{2,10},{4,12},{6,14},{8,0},{10,2},{12,4},{14,6},{16,24},{18,... | collective-permute-start | bytes 110600 | tf_op jit(solution)/shard_map/ppermute | solution.py:247
  6.4 20.4 %collective-permute-start.15 = (bf16[1,24,768]{2,1,0:T(8,128)(2,1)S(1)}, bf16[1,24,768]{2,1,0:T(8,128)(2,1)S(1)}, u32[]{:S(2)}, u32[]{:S(2)}) collective-permute-start(bf16[1,24,768]{2,1,0:T(8,128)(2,1)S(1)} %get-tuple-element.268), channel_id=1, source_target_pairs={{0,8},{2,10},{4,12},{6,14},{8,0},{10,2},{12,4},{14,6},{16,24},{18,... | collective-permute-start | bytes 110600 | tf_op jit(solution)/shard_map/ppermute | solution.py:247
  6.4 20.4 %collective-permute-start.30 = (bf16[1,24,768]{2,1,0:T(8,128)(2,1)S(1)}, bf16[1,24,768]{2,1,0:T(8,128)(2,1)S(1)}, u32[]{:S(2)}, u32[]{:S(2)}) collective-permute-start(bf16[1,24,768]{2,1,0:T(8,128)(2,1)S(1)} %get-tuple-element.267), channel_id=1, source_target_pairs={{0,8},{2,10},{4,12},{6,14},{8,0},{10,2},{12,4},{14,6},{16,24},{18,... | collective-permute-start | bytes 110600 | tf_op jit(solution)/shard_map/ppermute | solution.py:247
  8.6 19.7 %collective-permute-start.4 = (bf16[1,24,768]{2,1,0:T(8,128)(2,1)S(1)}, bf16[1,24,768]{2,1,0:T(8,128)(2,1)S(1)}, u32[]{:S(2)}, u32[]{:S(2)}) collective-permute-start(bf16[1,24,768]{2,1,0:T(8,128)(2,1)S(1)} %maximum_bitcast_fusion.30), channel_id=1, source_target_pairs={{0,8},{2,10},{4,12},{6,14},{8,0},{10,2},{12,4},{14,6},{16,24},{18,... | collective-permute-start | bytes 110600 | tf_op jit(solution)/shard_map/ppermute | solution.py:247
  26.9 18.6 %collective-permute-start.16 = (bf16[2,24,768]{2,1,0:T(8,128)(2,1)S(1)}, bf16[2,24,768]{2,1,0:T(8,128)(2,1)S(1)}, u32[]{:S(2)}, u32[]{:S(2)}) collective-permute-start(bf16[2,24,768]{2,1,0:T(8,128)(2,1)S(1)} %maximum_bitcast_fusion.26), channel_id=1, source_target_pairs={{0,16},{2,18},{4,20},{6,22},{8,24},{10,26},{12,28},{14,30},{16,0},... | collective-permute-start | bytes 221192 | tf_op jit(solution)/shard_map/ppermute | solution.py:247
  28.4 18.6 %collective-permute-start.5 = (bf16[2,24,768]{2,1,0:T(8,128)(2,1)S(1)}, bf16[2,24,768]{2,1,0:T(8,128)(2,1)S(1)}, u32[]{:S(2)}, u32[]{:S(2)}) collective-permute-start(bf16[2,24,768]{2,1,0:T(8,128)(2,1)S(1)} %maximum_bitcast_fusion.24), channel_id=1, source_target_pairs={{0,16},{2,18},{4,20},{6,22},{8,24},{10,26},{12,28},{14,30},{16,0},... | collective-permute-start | bytes 221192 | tf_op jit(solution)/shard_map/ppermute | solution.py:247
  30.1 17.0 %collective-permute-start.26 = (bf16[2,24,768]{2,1,0:T(8,128)(2,1)S(1)}, bf16[2,24,768]{2,1,0:T(8,128)(2,1)S(1)}, u32[]{:S(2)}, u32[]{:S(2)}) collective-permute-start(bf16[2,24,768]{2,1,0:T(8,128)(2,1)S(1)} %maximum_bitcast_fusion.28), channel_id=1, source_target_pairs={{0,16},{2,18},{4,20},{6,22},{8,24},{10,26},{12,28},{14,30},{16,0},... | collective-permute-start | bytes 221192 | tf_op jit(solution)/shard_map/ppermute | solution.py:247
  57.0 24.9 %collective-permute-start.18 = (bf16[8,24,768]{2,1,0:T(8,128)(2,1)}, bf16[8,24,768]{2,1,0:T(8,128)(2,1)}, u32[]{:S(2)}, u32[]{:S(2)}) collective-permute-start(bf16[8,24,768]{2,1,0:T(8,128)(2,1)} %bitcast.76), channel_id=1, source_target_pairs={{0,4},{2,6},{4,0},{6,2},{8,12},{10,14},{12,8},{14,10},{16,20},{18,... | collective-permute-start | bytes 884744 | tf_op jit(solution)/shard_map/ppermute | solution.py:247
  61.8 17.9 %collective-permute-start.23 = (bf16[8,24,768]{2,1,0:T(8,128)(2,1)S(1)}, bf16[8,24,768]{2,1,0:T(8,128)(2,1)S(1)}, u32[]{:S(2)}, u32[]{:S(2)}) collective-permute-start(bf16[8,24,768]{2,1,0:T(8,128)(2,1)S(1)} %bitcast.1059), channel_id=1, source_target_pairs={{0,4},{2,6},{4,0},{6,2},{8,12},{10,14},{12,8},{14,10},{16,20},{18,... | collective-permute-start | bytes 884744 | tf_op jit(solution)/shard_map/ppermute | solution.py:247
  63.2 21.3 %collective-permute-start.28 = (bf16[8,24,768]{2,1,0:T(8,128)(2,1)}, bf16[8,24,768]{2,1,0:T(8,128)(2,1)}, u32[]{:S(2)}, u32[]{:S(2)}) collective-permute-start(bf16[8,24,768]{2,1,0:T(8,128)(2,1)} %bitcast.121), channel_id=1, source_target_pairs={{0,2},{2,0},{4,6},{6,4},{8,10},{10,8},{12,14},{14,12},{16,18},{18,... | collective-permute-start | bytes 884744 | tf_op jit(solution)/shard_map/ppermute | solution.py:247
  64.6 22.0 %collective-permute-start.33 = (bf16[8,24,768]{2,1,0:T(8,128)(2,1)}, bf16[8,24,768]{2,1,0:T(8,128)(2,1)}, u32[]{:S(2)}, u32[]{:S(2)}) collective-permute-start(bf16[8,24,768]{2,1,0:T(8,128)(2,1)} %bitcast.140), channel_id=1, source_target_pairs={{0,4},{2,6},{4,0},{6,2},{8,12},{10,14},{12,8},{14,10},{16,20},{18,... | collective-permute-start | bytes 884744 | tf_op jit(solution)/shard_map/ppermute | solution.py:247
  81.9 43.9 %collective-permute-start.24 = (bf16[384,768]{1,0:T(8,128)(2,1)S(1)}, bf16[384,768]{1,0:T(8,128)(2,1)}, u32[]{:S(2)}, u32[]{:S(2)}) collective-permute-start(bf16[384,768]{1,0:T(8,128)(2,1)S(1)} %bitcast.1034), channel_id=1, source_target_pairs={{0,1},{1,0},{2,3},{3,2},{4,5},{5,4},{6,7},{7,6},{8,9},{9,8},{10,11... | collective-permute-start | bytes 1769480 | tf_op jit(solution)/shard_map/ppermute | solution.py:297
  84.5 96.1 %collective-permute-start.19 = (bf16[384,768]{1,0:T(8,128)(2,1)}, bf16[384,768]{1,0:T(8,128)(2,1)}, u32[]{:S(2)}, u32[]{:S(2)}) collective-permute-start(bf16[384,768]{1,0:T(8,128)(2,1)} %bitcast.81), channel_id=1, source_target_pairs={{0,1},{1,0},{2,3},{3,2},{4,5},{5,4},{6,7},{7,6},{8,9},{9,8},{10,11... | collective-permute-start | bytes 1769480 | tf_op jit(solution)/shard_map/ppermute | solution.py:297
  86.5 132.9 %collective-permute-start.29 = (bf16[384,768]{1,0:T(8,128)(2,1)}, bf16[384,768]{1,0:T(8,128)(2,1)}, u32[]{:S(2)}, u32[]{:S(2)}) collective-permute-start(bf16[384,768]{1,0:T(8,128)(2,1)} %bitcast.124), channel_id=1, source_target_pairs={{0,1},{1,0},{2,3},{3,2},{4,5},{5,4},{6,7},{7,6},{8,9},{9,8},{10,11... | collective-permute-start | bytes 1769480 | tf_op jit(solution)/shard_map/ppermute | solution.py:297
  89.0 161.0 %collective-permute-start.34 = (bf16[384,768]{1,0:T(8,128)(2,1)}, bf16[384,768]{1,0:T(8,128)(2,1)}, u32[]{:S(2)}, u32[]{:S(2)}) collective-permute-start(bf16[384,768]{1,0:T(8,128)(2,1)} %bitcast.145), channel_id=1, source_target_pairs={{0,1},{1,0},{2,3},{3,2},{4,5},{5,4},{6,7},{7,6},{8,9},{9,8},{10,11... | collective-permute-start | bytes 1769480 | tf_op jit(solution)/shard_map/ppermute | solution.py:297
  91.1 50.1 %collective-permute-start.14 = (bf16[384,768]{1,0:T(8,128)(2,1)}, bf16[384,768]{1,0:T(8,128)(2,1)}, u32[]{:S(2)}, u32[]{:S(2)}) collective-permute-start(bf16[384,768]{1,0:T(8,128)(2,1)} %bitcast.59), channel_id=1, source_target_pairs={{0,1},{1,0},{2,3},{3,2},{4,5},{5,4},{6,7},{7,6},{8,9},{9,8},{10,11... | collective-permute-start | bytes 1769480 | tf_op jit(solution)/shard_map/ppermute | solution.py:297
  424.6 18.5 %collective-permute-start.67 = (f32[16,24,128]{2,0,1:T(8,128)S(1)}, f32[16,24,128]{2,0,1:T(8,128)S(1)}, u32[]{:S(2)}, u32[]{:S(2)}) collective-permute-start(f32[16,24,128]{2,0,1:T(8,128)S(1)} %pad.38), channel_id=1, source_target_pairs={{0,1},{1,0},{2,3},{3,2},{4,5},{5,4},{6,7},{7,6},{8,9},{9,8},{10,11... | collective-permute-start | bytes 589832 | tf_op jit(solution)/shard_map/ppermute | solution.py:297
  433.2 51.5 %collective-permute-start.62 = (bf16[384,768]{1,0:T(8,128)(2,1)}, bf16[384,768]{1,0:T(8,128)(2,1)}, u32[]{:S(2)}, u32[]{:S(2)}) collective-permute-start(bf16[384,768]{1,0:T(8,128)(2,1)} %fusion.63), channel_id=1, source_target_pairs={{0,1},{1,0},{2,3},{3,2},{4,5},{5,4},{6,7},{7,6},{8,9},{9,8},{10,11... | collective-permute-start | bytes 1769480 | tf_op jit(solution)/shard_map/ppermute | solution.py:297
  450.2 32.6 %collective-permute-start.47 = (bf16[384,768]{1,0:T(8,128)(2,1)}, bf16[384,768]{1,0:T(8,128)(2,1)}, u32[]{:S(2)}, u32[]{:S(2)}) collective-permute-start(bf16[384,768]{1,0:T(8,128)(2,1)} %slice.1140), channel_id=1, source_target_pairs={{0,1},{1,0},{2,3},{3,2},{4,5},{5,4},{6,7},{7,6},{8,9},{9,8},{10,11... | collective-permute-start | bytes 1769480 | tf_op jit(solution)/shard_map/ppermute | solution.py:297
  458.3 16.6 %collective-permute-start.71 = (bf16[1,1,24,128]{2,3,1,0:T(8,128)(2,1)}, bf16[1,1,24,128]{2,3,1,0:T(8,128)(2,1)S(1)}, u32[]{:S(2)}, u32[]{:S(2)}) collective-permute-start(bf16[1,1,24,128]{2,3,1,0:T(8,128)(2,1)} %fusion.159), channel_id=1, source_target_pairs={{0,8},{2,10},{4,12},{6,14},{8,0},{10,2},{12,4},{14,6},{16,24},{18,... | collective-permute-start | bytes 18440 | tf_op jit(solution)/shard_map/ppermute | solution.py:247
  463.0 18.0 %collective-permute-start.57 = (bf16[384,768]{1,0:T(8,128)(2,1)}, bf16[384,768]{1,0:T(8,128)(2,1)S(1)}, u32[]{:S(2)}, u32[]{:S(2)}) collective-permute-start(bf16[384,768]{1,0:T(8,128)(2,1)} %fusion.62), channel_id=1, source_target_pairs={{0,1},{1,0},{2,3},{3,2},{4,5},{5,4},{6,7},{7,6},{8,9},{9,8},{10,11... | collective-permute-start | bytes 1769480 | tf_op jit(solution)/shard_map/ppermute | solution.py:297
  465.4 22.0 %collective-permute-start.52 = (bf16[384,768]{1,0:T(8,128)(2,1)}, bf16[384,768]{1,0:T(8,128)(2,1)}, u32[]{:S(2)}, u32[]{:S(2)}) collective-permute-start(bf16[384,768]{1,0:T(8,128)(2,1)} %slice.1139), channel_id=1, source_target_pairs={{0,1},{1,0},{2,3},{3,2},{4,5},{5,4},{6,7},{7,6},{8,9},{9,8},{10,11... | collective-permute-start | bytes 1769480 | tf_op jit(solution)/shard_map/ppermute | solution.py:297
  482.7 81.6 %collective-permute-start.36 = (f32[8,197,384]{2,0,1:T(8,128)}, f32[8,197,384]{2,0,1:T(8,128)}, u32[]{:S(2)}, u32[]{:S(2)}) collective-permute-start(f32[8,197,384]{2,0,1:T(8,128)} %copy.710), channel_id=1, source_target_pairs={{0,1},{1,0},{2,3},{3,2},{4,5},{5,4},{6,7},{7,6},{8,9},{9,8},{10,11... | collective-permute-start | bytes 7262216 | tf_op jit(solution)/shard_map/ppermute | solution.py:297
  484.7 85.3 %collective-permute-start.35 = (f32[8,197,384]{2,0,1:T(8,128)}, f32[8,197,384]{2,0,1:T(8,128)}, u32[]{:S(2)}, u32[]{:S(2)}) collective-permute-start(f32[8,197,384]{2,0,1:T(8,128)} %copy.692), channel_id=1, source_target_pairs={{0,1},{1,0},{2,3},{3,2},{4,5},{5,4},{6,7},{7,6},{8,9},{9,8},{10,11... | collective-permute-start | bytes 7262216 | tf_op jit(solution)/shard_map/ppermute | solution.py:297
  (187 other events, 2074.8 us)
